TPU v7x, 32 devices: a whole 2x2x4 slice. The times are simulated.
32 devices in a mesh: samp: 4 (over x, core), pos: 8 (over z, y).
Axes of the slice: x: 2, y: 2, z: 4, core: 2. Of those that a mesh axis runs over, the one named last changes fastest.
Arguments:
- dosages: bfloat16 [16384, 8192], P('samp', 'pos'), may hold values from -64 to 64
- phenotypes: bfloat16 [16384, 3072], P('samp', 'pos'), may hold values from -64 to 64
- window_low: int32 [3072], P('pos'), may hold values from 0 to 8191, as said below
- window_high: int32 [3072], P('pos'), may hold values from 0 to 8191, as said below
Outputs:
- statistics: float32 [8, 2048, 384], P('pos', 'samp')
Inputs may be any that keep to these rules, and one draw needn't show every extreme that they name: For peak p in block b = p // 384: b * 1024 - 512 <= window_low[p] <= window_high[p] <= b * 1024 + 1535. In every block but the first, one window starts exactly 512 variants before the block; in every block but the last, one ends exactly 512 variants after it. Same bounds as window_low; window_high[p] >= window_low[p].
All inputs are finite; a program needn't handle non-finite values.
Results may differ from a plain program's by a relative error of at most 0.0003.
Values may be sent and summed in bfloat16 or wider, within the bound.
No kernel may reach another device: no remote copies, remote signals or barrier semaphores. Data moves between devices by JAX's collectives and lax.ppermute only.
A program may use at most 64 MiB of HBM per device.

v0:
```python
import math
import jax
import jax.numpy as jnp
from jax import lax
from jax.sharding import PartitionSpec as P

HALO = 512
EPS = 1e-06


def padded(cells, sides, width):
    for axis, dim in sides:
        count = lax.axis_size(axis)
        ends = count - 1
        head = lax.slice_in_dim(cells, 0, width, axis=dim)
        tail = lax.slice_in_dim(cells, cells.shape[dim] - width, cells.shape[dim], axis=dim)
        cells = jnp.concatenate(
            [
                lax.ppermute(tail, axis, [(i, (i + 1) % count) for i in range(ends)]),
                cells,
                lax.ppermute(head, axis, [((i + 1) % count, i) for i in range(ends)]),
            ],
            axis=dim,
        )
    return cells


def from_behind(array, axis, by):
    devices = lax.axis_size(axis)
    pairs = [(i, i + by) for i in range(devices) if 0 <= i + by < devices]
    return lax.ppermute(array, axis, pairs)


def sum_squares(values):
    return jnp.sum(jnp.square(values.astype(jnp.float32)), axis=0)


def cross_rows(variant_panel, phenotypes):
    return lax.dot_general(
        variant_panel, phenotypes, (((0,), (0,)), ((), ())), preferred_element_type=jnp.float32
    )


def shards(dosages, phenotypes, window_low, window_high):
    sample_rows, block_width = dosages.shape
    peak_width = phenotypes.shape[1]
    span_width = block_width + 2 * HALO
    samp_count = lax.axis_size("samp")
    samp_index = lax.axis_index("samp")
    pos_index = lax.axis_index("pos")
    share_rows = span_width // samp_count
    own_first = samp_index * share_rows
    peak_squares = sum_squares(phenotypes)
    near_peaks = padded(phenotypes, (("pos", 1),), peak_width)
    own_tile = cross_rows(dosages, phenotypes)
    lower_edge = cross_rows(dosages[:, :HALO], near_peaks[:, :peak_width])
    upper_edge = cross_rows(dosages[:, block_width - HALO :], near_peaks[:, 2 * peak_width :])
    from_below = from_behind(upper_edge, "pos", 1)
    from_above = from_behind(lower_edge, "pos", -1)
    assembled = jnp.concatenate([from_below, own_tile, from_above], axis=0)
    owned_squares, peak_total = lax.psum((sum_squares(dosages), peak_squares), "samp")
    variant_total = padded(owned_squares, (("pos", 0),), HALO)
    cross_total = lax.psum(assembled, "samp")
    cross_share = lax.dynamic_slice_in_dim(cross_total, own_first, share_rows, 0)
    variant_share = lax.dynamic_slice_in_dim(variant_total, own_first, share_rows, 0)
    variant_index = (
        pos_index * block_width
        - HALO
        + own_first
        + jnp.arange(share_rows, dtype=jnp.int32)[:, None]
    )
    inside = (variant_index >= window_low[None, :]) & (variant_index <= window_high[None, :])
    factor = math.sqrt(float(sample_rows * samp_count - 2))
    scale_terms = (variant_share[:, None] + EPS) * (peak_total[None, :] + EPS)
    statistic = factor * cross_share / jnp.sqrt(scale_terms)
    return jnp.where(inside, statistic, jnp.zeros_like(statistic))[None]


def solution(mesh):
    placed = (P("samp", "pos"), P("samp", "pos"), P("pos"), P("pos"))
    return jax.shard_map(
        shards, mesh=mesh, in_specs=placed, out_specs=P("pos", "samp", None), check_vma=False
    )
```

profile of v0, /device:TPU:0, one launch (start us, length us, event | category | flops | bytes accessed | tf_op | source)
XLA Modules:
  0.0 270.4 jit_solution(13024341628665601439)
XLA Ops:
  6.5 0.0 all-reduce.3.cloned.1.call-start
  6.5 0.0 copy-start
  6.5 5.4 %collective-permute-start.2 = (bf16[4096,384]{1,0:T(8,128)(2,1)}, bf16[4096,384]{1,0:T(8,128)(2,1)S(1)}, u32[]{:S(2)}, u32[]{:S(2)}) collective-permute-start(bf16[4096,384]{1,0:T(8,128)(2,1)} %param.5), channel_id=1, source_target_pairs={{0,1},{1,2},{2,3},{3,4},{4,5},{5,6},{6,7},{8,9},{9,10},{10,11},{11... | collective-permute-start | bytes 9437192 | tf_op jit(solution)/shard_map/ppermute | solution.py:19
  11.9 1.3 collective-permute-start
  13.2 133.6 %collective-permute-done.2 = bf16[4096,384]{1,0:T(8,128)(2,1)S(1)} collective-permute-done((bf16[4096,384]{1,0:T(8,128)(2,1)}, bf16[4096,384]{1,0:T(8,128)(2,1)S(1)}, u32[]{:S(2)}, u32[]{:S(2)}) %collective-permute-start.2) | collective-permute-done | bytes 3145760 | tf_op jit(solution)/shard_map/ppermute | solution.py:19
  146.8 4.5 %fusion = f32[512,384]{1,0:T(8,128)S(1)} fusion(bf16[4096,384]{1,0:T(8,128)(2,1)S(1)} %collective-permute-done.2, bf16[4096,1024]{1,0:T(8,128)(2,1)} %param.4), kind=kOutput, calls=%fused_computation.2 | convolution fusion | flops 1610612736 | bytes 8126464 | tf_op jit(solution)/shard_map/dot_general | solution.py:39
  151.3 0.0 copy-start.1
  151.3 1.6 collective-permute-start.3
  152.9 0.0 collective-permute-done
  152.9 0.0 copy-done
  152.9 2.4 fusion.2
  155.3 5.0 %collective-permute-start.1 = (f32[512,384]{1,0:T(8,128)S(1)}, f32[512,384]{1,0:T(8,128)S(1)}, u32[]{:S(2)}, u32[]{:S(2)}) collective-permute-start(f32[512,384]{1,0:T(8,128)S(1)} %fusion.2), channel_id=1, source_target_pairs={{0,1},{1,2},{2,3},{3,4},{4,5},{5,6},{6,7},{8,9},{9,10},{10,11},{11... | collective-permute-start | bytes 2359304 | tf_op jit(solution)/shard_map/ppermute | solution.py:31
  160.3 0.0 copy-done.1
  160.3 4.5 %fusion.8 = f32[1024,384]{1,0:T(8,128)S(1)} fusion(bf16[4096,1024]{1,0:T(8,128)(2,1)S(1)} %copy-done, bf16[4096,384]{1,0:T(8,128)(2,1)S(1)} %copy-done.1), kind=kOutput, calls=%fused_computation.17 | convolution fusion | flops 3221225472 | bytes 13107200 | tf_op jit(solution)/shard_map/dot_general | solution.py:39
  164.8 7.7 %collective-permute-done.3 = f32[512,384]{1,0:T(8,128)S(1)} collective-permute-done((f32[512,384]{1,0:T(8,128)S(1)}, f32[512,384]{1,0:T(8,128)S(1)}, u32[]{:S(2)}, u32[]{:S(2)}) %collective-permute-start.3) | collective-permute-done | bytes 786464 | tf_op jit(solution)/shard_map/ppermute | solution.py:31
  172.6 17.0 %collective-permute-done.1 = f32[512,384]{1,0:T(8,128)S(1)} collective-permute-done((f32[512,384]{1,0:T(8,128)S(1)}, f32[512,384]{1,0:T(8,128)S(1)}, u32[]{:S(2)}, u32[]{:S(2)}) %collective-permute-start.1) | collective-permute-done | bytes 786464 | tf_op jit(solution)/shard_map/ppermute | solution.py:31
  189.6 1.9 pad_maximum_fusion
  191.4 0.0 all-reduce.3.cloned.1.call-update
  191.4 0.8 multiply_reduce_fusion.1
  192.2 0.0 copy-start.2
  192.2 0.0 copy-start.3
  192.2 5.1 %multiply_reduce_fusion = f32[1024]{0:T(1024)S(1)} fusion(bf16[4096,1024]{1,0:T(8,128)(2,1)} %param.4), kind=kLoop, calls=%fused_computation | loop fusion | flops 12581888 | bytes 8392704 | tf_op jit(solution)/shard_map/reduce_sum | solution.py:35
  197.3 7.8 %all-reduce = (f32[384]{0:T(512)S(1)}, f32[1024]{0:T(1024)S(1)}) all-reduce(f32[384]{0:T(512)S(1)} %multiply_reduce_fusion.1, f32[1024]{0:T(1024)S(1)} %multiply_reduce_fusion), channel_id=1, replica_groups=mesh['samp'=4,'pos'=8] {'samp'}, use_global_device_ids=true, to_apply=%region_4.0 | all-reduce | flops 1408 | bytes 11264 | tf_op jit(solution)/shard_map/psum | solution.py:61
  205.1 4.4 %collective-permute-start.4 = (f32[512]{0:T(512)S(1)}, f32[512]{0:T(512)S(1)}, u32[]{:S(2)}, u32[]{:S(2)}) collective-permute-start(f32[512]{0:T(512)S(1)} %get-tuple-element.8), channel_id=1, source_target_pairs={{0,1},{1,2},{2,3},{3,4},{4,5},{5,6},{6,7},{8,9},{9,10},{10,11},{11... | collective-permute-start | bytes 6152 | tf_op jit(solution)/shard_map/ppermute | solution.py:19
  209.5 1.3 collective-permute-start.5
  210.9 0.0 collective-permute-done.4
  210.9 4.1 %collective-permute-done.5 = f32[512]{0:T(512)S(1)} collective-permute-done((f32[512]{0:T(512)S(1)}, f32[512]{0:T(512)S(1)}, u32[]{:S(2)}, u32[]{:S(2)}) %collective-permute-start.5) | collective-permute-done | bytes 2080 | tf_op jit(solution)/shard_map/ppermute | solution.py:21
  215.0 0.1 fusion.6
  215.1 46.1 %all-reduce.3.cloned.1.call-done = f32[2048,384]{1,0:T(8,128)} async-done(((f32[2048,384]{1,0:T(8,128)}), f32[2048,384]{1,0:T(8,128)}) %all-reduce.3.cloned.1.call-update) | async-done | bytes 3145744 | tf_op jit(solution)/shard_map/psum | solution.py:63
  261.2 0.0 copy-done.2
  261.2 0.0 copy-done.3
  261.2 2.3 select_bitcast_fusion
  (3 shorter events, 0.0 us)
Async XLA Ops:
  6.5 254.7 %all-reduce.3.cloned.1.call-start = ((), (), s32[]{:S(2)}) async-start(), calls=%async_computation | async-start | bytes 6291456 | tf_op jit(solution)/shard_map/psum | solution.py:63
  6.5 146.4 %copy-start = (bf16[4096,1024]{1,0:T(8,128)(2,1)S(1)}, bf16[4096,1024]{1,0:T(8,128)(2,1)}, u32[]{:S(2)}) copy-start(bf16[4096,1024]{1,0:T(8,128)(2,1)} %param.4) | copy-start | bytes 25165828
  6.5 140.2 %collective-permute-start.2 = (bf16[4096,384]{1,0:T(8,128)(2,1)}, bf16[4096,384]{1,0:T(8,128)(2,1)S(1)}, u32[]{:S(2)}, u32[]{:S(2)}) collective-permute-start(bf16[4096,384]{1,0:T(8,128)(2,1)} %param.5), channel_id=1, source_target_pairs={{0,1},{1,2},{2,3},{3,4},{4,5},{5,6},{6,7},{8,9},{9,10},{10,11},{11... | collective-permute-start | bytes 9437192 | tf_op jit(solution)/shard_map/ppermute | solution.py:19
  11.9 141.0 %collective-permute-start = (bf16[4096,384]{1,0:T(8,128)(2,1)}, bf16[4096,384]{1,0:T(8,128)(2,1)S(1)}, u32[]{:S(2)}, u32[]{:S(2)}) collective-permute-start(bf16[4096,384]{1,0:T(8,128)(2,1)} %param.5), channel_id=1, source_target_pairs={{1,0},{2,1},{3,2},{4,3},{5,4},{6,5},{7,6},{9,8},{10,9},{11,10},{12... | collective-permute-start | bytes 9437192 | tf_op jit(solution)/shard_map/ppermute | solution.py:21
  151.3 9.0 %copy-start.1 = (bf16[4096,384]{1,0:T(8,128)(2,1)S(1)}, bf16[4096,384]{1,0:T(8,128)(2,1)}, u32[]{:S(2)}) copy-start(bf16[4096,384]{1,0:T(8,128)(2,1)} %param.5) | copy-start | bytes 9437188
  151.3 21.2 %collective-permute-start.3 = (f32[512,384]{1,0:T(8,128)S(1)}, f32[512,384]{1,0:T(8,128)S(1)}, u32[]{:S(2)}, u32[]{:S(2)}) collective-permute-start(f32[512,384]{1,0:T(8,128)S(1)} %fusion), channel_id=1, source_target_pairs={{1,0},{2,1},{3,2},{4,3},{5,4},{6,5},{7,6},{9,8},{10,9},{11,10},{12... | collective-permute-start | bytes 2359304 | tf_op jit(solution)/shard_map/ppermute | solution.py:31
  155.3 34.2 %collective-permute-start.1 = (f32[512,384]{1,0:T(8,128)S(1)}, f32[512,384]{1,0:T(8,128)S(1)}, u32[]{:S(2)}, u32[]{:S(2)}) collective-permute-start(f32[512,384]{1,0:T(8,128)S(1)} %fusion.2), channel_id=1, source_target_pairs={{0,1},{1,2},{2,3},{3,4},{4,5},{5,6},{6,7},{8,9},{9,10},{10,11},{11... | collective-permute-start | bytes 2359304 | tf_op jit(solution)/shard_map/ppermute | solution.py:31
  192.2 69.0 %copy-start.2 = (s32[384]{0:T(512)S(1)}, s32[384]{0:T(512)}, u32[]{:S(2)}) copy-start(s32[384]{0:T(512)} %param.7) | copy-start | bytes 4612
  192.2 69.0 %copy-start.3 = (s32[384]{0:T(512)S(1)}, s32[384]{0:T(512)}, u32[]{:S(2)}) copy-start(s32[384]{0:T(512)} %param.6) | copy-start | bytes 4612
  205.1 5.7 %collective-permute-start.4 = (f32[512]{0:T(512)S(1)}, f32[512]{0:T(512)S(1)}, u32[]{:S(2)}, u32[]{:S(2)}) collective-permute-start(f32[512]{0:T(512)S(1)} %get-tuple-element.8), channel_id=1, source_target_pairs={{0,1},{1,2},{2,3},{3,4},{4,5},{5,6},{6,7},{8,9},{9,10},{10,11},{11... | collective-permute-start | bytes 6152 | tf_op jit(solution)/shard_map/ppermute | solution.py:19
  209.5 5.5 %collective-permute-start.5 = (f32[512]{0:T(512)S(1)}, f32[512]{0:T(512)S(1)}, u32[]{:S(2)}, u32[]{:S(2)}) collective-permute-start(f32[512]{0:T(512)S(1)} %get-tuple-element.7), channel_id=1, source_target_pairs={{1,0},{2,1},{3,2},{4,3},{5,4},{6,5},{7,6},{9,8},{10,9},{11,10},{12... | collective-permute-start | bytes 6152 | tf_op jit(solution)/shard_map/ppermute | solution.py:21
Sparse Core Ops, SparseCore 0:
  191.6 69.6 all-reduce.2
where the time goes:
time: 271 us; the launch traced here: 270 us
  waiting for transfers between devices  209 us (77%)
  starting transfers between devices  18.8 us (7%)
  between operations  13.5 us (5%)
  matrix products  11.5 us (4%)
  other arithmetic  10.1 us (4%)
  blocking collectives  7.8 us (3%)
    ppermute x2, waiting for transfers between devices, padded(): lax.ppermute(tail, axis, [(i, (i + 1) % count) for i in range(ends)])  134 us
    psum x1, waiting for transfers between devices, shards(): cross_total = lax.psum(assembled, 'samp')  46.1 us
    ppermute x2, waiting for transfers between devices, from_behind(): return lax.ppermute(array, axis, pairs)  24.7 us
    dot_general x3, matrix products, cross_rows(): lax.dot_general(variant_panel, phenotypes, (((0,), (0,)), ((), ())), pref...  11.5 us
    ppermute x2, starting transfers between devices, padded(): lax.ppermute(tail, axis, [(i, (i + 1) % count) for i in range(ends)])  9.74 us
    psum x1, blocking collectives, shards(): lax.psum((sum_squares(dosages), peak_squares), 'samp')  7.8 us
    ppermute x2, starting transfers between devices, from_behind(): return lax.ppermute(array, axis, pairs)  6.51 us
    reduce_sum x2, other arithmetic, sum_squares(): return jnp.sum(jnp.square(values.astype(jnp.float32)), axis=0)  5.86 us
  transfers between devices with their start and end apart: 7, of which 5 were waited for; matrix products, arithmetic and copies ran while one was open for 6% of the time, Pallas kernels for 0%

commit v1 on v0

--- a/solution.py
+++ b/solution.py
@@ -6,6 +6,7 @@
 
 HALO = 512
 EPS = 1e-06
+expand_shifts_all = lambda x0: jnp.sum(lax.all_gather(x0, "samp"), 0)
 
 
 def padded(cells, sides, width):
@@ -60,7 +61,7 @@
     assembled = jnp.concatenate([from_below, own_tile, from_above], axis=0)
     owned_squares, peak_total = lax.psum((sum_squares(dosages), peak_squares), "samp")
     variant_total = padded(owned_squares, (("pos", 0),), HALO)
-    cross_total = lax.psum(assembled, "samp")
+    cross_total = expand_shifts_all(assembled)
     cross_share = lax.dynamic_slice_in_dim(cross_total, own_first, share_rows, 0)
     variant_share = lax.dynamic_slice_in_dim(variant_total, own_first, share_rows, 0)
     variant_index = (

time: 271 us -> 289 us (1.066)
  waiting for transfers between devices: 209 us -> 223 us
  other arithmetic: 10.1 us -> 14.5 us
    all_gather x0 -> x1, waiting for transfers between devices: none -> 60.7 us  [expand_shifts_all = lambda x0: jnp.sum(lax.all_gather(x0, 'samp'), 0)]
    psum x1 -> x0, waiting for transfers between devices: 46.1 us -> none  [shards(): cross_total = lax.psum(assembled, 'samp')]
    reduce_sum x0 -> x1, other arithmetic: none -> 5.6 us  [expand_shifts_all = lambda x0: jnp.sum(lax.all_gather(x0, 'samp'), 0)]
where the time goes in v1:
time: 289 us; the launch traced here: 288 us
  waiting for transfers between devices  223 us (77%)
  starting transfers between devices  18.8 us (7%)
  other arithmetic  14.5 us (5%)
  between operations  13.5 us (5%)
  matrix products  11.5 us (4%)
  blocking collectives  6.96 us (2%)
    ppermute x2, waiting for transfers between devices, padded(): lax.ppermute(tail, axis, [(i, (i + 1) % count) for i in range(ends)])  134 us
    all_gather x1, waiting for transfers between devices, expand_shifts_all = lambda x0: jnp.sum(lax.all_gather(x0, 'samp'), 0)  60.7 us
    ppermute x2, waiting for transfers between devices, from_behind(): return lax.ppermute(array, axis, pairs)  24.7 us
    dot_general x3, matrix products, cross_rows(): lax.dot_general(variant_panel, phenotypes, (((0,), (0,)), ((), ())), pref...  11.5 us
    ppermute x2, starting transfers between devices, padded(): lax.ppermute(tail, axis, [(i, (i + 1) % count) for i in range(ends)])  9.74 us
    psum x1, blocking collectives, shards(): lax.psum((sum_squares(dosages), peak_squares), 'samp')  6.96 us
    ppermute x2, starting transfers between devices, from_behind(): return lax.ppermute(array, axis, pairs)  6.51 us
    reduce_sum x2, other arithmetic, sum_squares(): return jnp.sum(jnp.square(values.astype(jnp.float32)), axis=0)  5.84 us
  transfers between devices with their start and end apart: 7, of which 5 were waited for; matrix products, arithmetic and copies ran while one was open for 6% of the time, Pallas kernels for 0%

profile of v1, /device:TPU:0, one launch (start us, length us, event | category | flops | bytes accessed | tf_op | source)
XLA Modules:
  0.0 288.5 jit_solution(3672579936347686011)
XLA Ops:
  6.5 0.0 all-gather.3.cloned.1.call-start
  6.5 0.0 copy-start
  6.5 5.4 %collective-permute-start.2 = (bf16[4096,384]{1,0:T(8,128)(2,1)}, bf16[4096,384]{1,0:T(8,128)(2,1)S(1)}, u32[]{:S(2)}, u32[]{:S(2)}) collective-permute-start(bf16[4096,384]{1,0:T(8,128)(2,1)} %param.5), channel_id=1, source_target_pairs={{0,1},{1,2},{2,3},{3,4},{4,5},{5,6},{6,7},{8,9},{9,10},{10,11},{11... | collective-permute-start | bytes 9437192 | tf_op jit(solution)/shard_map/ppermute | solution.py:20
  11.9 1.3 collective-permute-start
  13.2 133.6 %collective-permute-done.2 = bf16[4096,384]{1,0:T(8,128)(2,1)S(1)} collective-permute-done((bf16[4096,384]{1,0:T(8,128)(2,1)}, bf16[4096,384]{1,0:T(8,128)(2,1)S(1)}, u32[]{:S(2)}, u32[]{:S(2)}) %collective-permute-start.2) | collective-permute-done | bytes 3145760 | tf_op jit(solution)/shard_map/ppermute | solution.py:20
  146.8 4.5 %fusion = f32[512,384]{1,0:T(8,128)S(1)} fusion(bf16[4096,384]{1,0:T(8,128)(2,1)S(1)} %collective-permute-done.2, bf16[4096,1024]{1,0:T(8,128)(2,1)} %param.4), kind=kOutput, calls=%fused_computation.2 | convolution fusion | flops 1610612736 | bytes 8126464 | tf_op jit(solution)/shard_map/dot_general | solution.py:40
  151.3 0.0 copy-start.1
  151.3 1.6 collective-permute-start.3
  152.9 0.0 collective-permute-done
  152.9 0.0 copy-done
  152.9 2.4 fusion.2
  155.3 5.0 %collective-permute-start.1 = (f32[512,384]{1,0:T(8,128)S(1)}, f32[512,384]{1,0:T(8,128)S(1)}, u32[]{:S(2)}, u32[]{:S(2)}) collective-permute-start(f32[512,384]{1,0:T(8,128)S(1)} %fusion.2), channel_id=1, source_target_pairs={{0,1},{1,2},{2,3},{3,4},{4,5},{5,6},{6,7},{8,9},{9,10},{10,11},{11... | collective-permute-start | bytes 2359304 | tf_op jit(solution)/shard_map/ppermute | solution.py:32
  160.3 0.0 copy-done.1
  160.3 4.5 %fusion.8 = f32[1024,384]{1,0:T(8,128)S(1)} fusion(bf16[4096,1024]{1,0:T(8,128)(2,1)S(1)} %copy-done, bf16[4096,384]{1,0:T(8,128)(2,1)S(1)} %copy-done.1), kind=kOutput, calls=%fused_computation.17 | convolution fusion | flops 3221225472 | bytes 13107200 | tf_op jit(solution)/shard_map/dot_general | solution.py:40
  164.8 7.7 %collective-permute-done.3 = f32[512,384]{1,0:T(8,128)S(1)} collective-permute-done((f32[512,384]{1,0:T(8,128)S(1)}, f32[512,384]{1,0:T(8,128)S(1)}, u32[]{:S(2)}, u32[]{:S(2)}) %collective-permute-start.3) | collective-permute-done | bytes 786464 | tf_op jit(solution)/shard_map/ppermute | solution.py:32
  172.6 17.0 %collective-permute-done.1 = f32[512,384]{1,0:T(8,128)S(1)} collective-permute-done((f32[512,384]{1,0:T(8,128)S(1)}, f32[512,384]{1,0:T(8,128)S(1)}, u32[]{:S(2)}, u32[]{:S(2)}) %collective-permute-start.1) | collective-permute-done | bytes 786464 | tf_op jit(solution)/shard_map/ppermute | solution.py:32
  189.6 1.9 pad_maximum_fusion
  191.4 0.0 all-gather.3.cloned.1.call-update
  191.4 0.8 multiply_reduce_fusion.1
  192.2 5.1 %multiply_reduce_fusion = f32[1024]{0:T(1024)S(1)} fusion(bf16[4096,1024]{1,0:T(8,128)(2,1)} %param.4), kind=kLoop, calls=%fused_computation | loop fusion | flops 12581888 | bytes 8392704 | tf_op jit(solution)/shard_map/reduce_sum | solution.py:36
  197.3 7.0 %all-reduce = (f32[384]{0:T(512)S(1)}, f32[1024]{0:T(1024)S(1)}) all-reduce(f32[384]{0:T(512)S(1)} %multiply_reduce_fusion.1, f32[1024]{0:T(1024)S(1)} %multiply_reduce_fusion), channel_id=1, replica_groups=mesh['samp'=4,'pos'=8] {'samp'}, use_global_device_ids=true, to_apply=%region_4.0 | all-reduce | flops 1408 | bytes 11264 | tf_op jit(solution)/shard_map/psum | solution.py:62
  204.3 4.4 %collective-permute-start.4 = (f32[512]{0:T(512)S(1)}, f32[512]{0:T(512)S(1)}, u32[]{:S(2)}, u32[]{:S(2)}) collective-permute-start(f32[512]{0:T(512)S(1)} %get-tuple-element.8), channel_id=1, source_target_pairs={{0,1},{1,2},{2,3},{3,4},{4,5},{5,6},{6,7},{8,9},{9,10},{10,11},{11... | collective-permute-start | bytes 6152 | tf_op jit(solution)/shard_map/ppermute | solution.py:20
  208.6 1.3 collective-permute-start.5
  210.0 0.0 collective-permute-done.4
  210.0 4.1 %collective-permute-done.5 = f32[512]{0:T(512)S(1)} collective-permute-done((f32[512]{0:T(512)S(1)}, f32[512]{0:T(512)S(1)}, u32[]{:S(2)}, u32[]{:S(2)}) %collective-permute-start.5) | collective-permute-done | bytes 2080 | tf_op jit(solution)/shard_map/ppermute | solution.py:22
  214.1 0.1 fusion.6
  214.2 60.7 %all-gather.3.cloned.1.call-done = f32[8192,384]{1,0:T(8,128)} async-done(((f32[2048,384]{1,0:T(8,128)}), f32[8192,384]{1,0:T(8,128)}) %all-gather.3.cloned.1.call-update) | async-done | bytes 12582928 | tf_op jit(solution)/shard_map/all_gather | solution.py:9
  274.9 0.0 copy-start.2
  274.9 0.0 copy-start.3
  274.9 5.6 %reduce_sum.27 = f32[2048,384]{1,0:T(8,128)S(1)} reduce(f32[4,2048,384]{2,1,0:T(8,128)} %bitcast.7, f32[]{:T(128)} %constant.7.clone.1), dimensions={0}, to_apply=%region_0.0 | reduce | flops 2359296 | bytes 15728644 | tf_op jit(solution)/shard_map/reduce_sum | solution.py:9
  280.5 0.0 copy-done.2
  280.5 0.0 copy-done.3
  280.5 1.2 select_bitcast_fusion
  (3 shorter events, 0.0 us)
Async XLA Ops:
  6.5 268.3 %all-gather.3.cloned.1.call-start = ((), (), s32[]{:S(2)}) async-start(), calls=%async_computation | async-start | bytes 15728640 | tf_op jit(solution)/shard_map/all_gather | solution.py:9
  6.5 146.4 %copy-start = (bf16[4096,1024]{1,0:T(8,128)(2,1)S(1)}, bf16[4096,1024]{1,0:T(8,128)(2,1)}, u32[]{:S(2)}) copy-start(bf16[4096,1024]{1,0:T(8,128)(2,1)} %param.4) | copy-start | bytes 25165828
  6.5 140.2 %collective-permute-start.2 = (bf16[4096,384]{1,0:T(8,128)(2,1)}, bf16[4096,384]{1,0:T(8,128)(2,1)S(1)}, u32[]{:S(2)}, u32[]{:S(2)}) collective-permute-start(bf16[4096,384]{1,0:T(8,128)(2,1)} %param.5), channel_id=1, source_target_pairs={{0,1},{1,2},{2,3},{3,4},{4,5},{5,6},{6,7},{8,9},{9,10},{10,11},{11... | collective-permute-start | bytes 9437192 | tf_op jit(solution)/shard_map/ppermute | solution.py:20
  11.9 141.0 %collective-permute-start = (bf16[4096,384]{1,0:T(8,128)(2,1)}, bf16[4096,384]{1,0:T(8,128)(2,1)S(1)}, u32[]{:S(2)}, u32[]{:S(2)}) collective-permute-start(bf16[4096,384]{1,0:T(8,128)(2,1)} %param.5), channel_id=1, source_target_pairs={{1,0},{2,1},{3,2},{4,3},{5,4},{6,5},{7,6},{9,8},{10,9},{11,10},{12... | collective-permute-start | bytes 9437192 | tf_op jit(solution)/shard_map/ppermute | solution.py:22
  151.3 9.0 %copy-start.1 = (bf16[4096,384]{1,0:T(8,128)(2,1)S(1)}, bf16[4096,384]{1,0:T(8,128)(2,1)}, u32[]{:S(2)}) copy-start(bf16[4096,384]{1,0:T(8,128)(2,1)} %param.5) | copy-start | bytes 9437188
  151.3 21.2 %collective-permute-start.3 = (f32[512,384]{1,0:T(8,128)S(1)}, f32[512,384]{1,0:T(8,128)S(1)}, u32[]{:S(2)}, u32[]{:S(2)}) collective-permute-start(f32[512,384]{1,0:T(8,128)S(1)} %fusion), channel_id=1, source_target_pairs={{1,0},{2,1},{3,2},{4,3},{5,4},{6,5},{7,6},{9,8},{10,9},{11,10},{12... | collective-permute-start | bytes 2359304 | tf_op jit(solution)/shard_map/ppermute | solution.py:32
  155.3 34.2 %collective-permute-start.1 = (f32[512,384]{1,0:T(8,128)S(1)}, f32[512,384]{1,0:T(8,128)S(1)}, u32[]{:S(2)}, u32[]{:S(2)}) collective-permute-start(f32[512,384]{1,0:T(8,128)S(1)} %fusion.2), channel_id=1, source_target_pairs={{0,1},{1,2},{2,3},{3,4},{4,5},{5,6},{6,7},{8,9},{9,10},{10,11},{11... | collective-permute-start | bytes 2359304 | tf_op jit(solution)/shard_map/ppermute | solution.py:32
  204.3 5.7 %collective-permute-start.4 = (f32[512]{0:T(512)S(1)}, f32[512]{0:T(512)S(1)}, u32[]{:S(2)}, u32[]{:S(2)}) collective-permute-start(f32[512]{0:T(512)S(1)} %get-tuple-element.8), channel_id=1, source_target_pairs={{0,1},{1,2},{2,3},{3,4},{4,5},{5,6},{6,7},{8,9},{9,10},{10,11},{11... | collective-permute-start | bytes 6152 | tf_op jit(solution)/shard_map/ppermute | solution.py:20
  208.6 5.5 %collective-permute-start.5 = (f32[512]{0:T(512)S(1)}, f32[512]{0:T(512)S(1)}, u32[]{:S(2)}, u32[]{:S(2)}) collective-permute-start(f32[512]{0:T(512)S(1)} %get-tuple-element.7), channel_id=1, source_target_pairs={{1,0},{2,1},{3,2},{4,3},{5,4},{6,5},{7,6},{9,8},{10,9},{11,10},{12... | collective-permute-start | bytes 6152 | tf_op jit(solution)/shard_map/ppermute | solution.py:22
  274.9 5.6 %copy-start.2 = (s32[384]{0:T(512)S(1)}, s32[384]{0:T(512)}, u32[]{:S(2)}) copy-start(s32[384]{0:T(512)} %param.7) | copy-start | bytes 4612
  274.9 5.6 %copy-start.3 = (s32[384]{0:T(512)S(1)}, s32[384]{0:T(512)}, u32[]{:S(2)}) copy-start(s32[384]{0:T(512)} %param.6) | copy-start | bytes 4612
Sparse Core Ops, SparseCore 0:
  191.6 83.2 all-gather.2
